TPU v7x, 32 devices: a whole 2x2x4 slice. The times are simulated.
32 devices in a mesh: scan: 4 (over z), tx: 4 (over y, x), ty: 2 (over core).
Axes of the slice: x: 2, y: 2, z: 4, core: 2. Of those that a mesh axis runs over, the one named last changes fastest.
Arguments:
- object_slices: float32 [2, 2, 1024, 512], P(None, None, 'tx', 'ty'), may hold values from -0.9 to 0.9
- probe_modes: float32 [2, 8, 256, 256], replicated, may hold values from -1.2 to 1.2
- corners: int32 [4, 2, 4, 2], P('tx', 'ty', 'scan'), may hold values from 0 to 127, as said below
- measured: float32 [4, 2, 4, 256, 256], P('tx', 'ty', 'scan'), may hold values from 0.2 to 2.5
Outputs:
- updated_object: float32 [2, 2, 1024, 512], P(None, None, 'tx', 'ty')
Inputs may be any that keep to these rules, and one draw needn't show every extreme that they name: corners place every window inside its own tile and the 128 pixels below and to the right of it.
All inputs are finite; a program needn't handle non-finite values.
Results may differ from a plain program's by a relative error of at most 0.0001.
Values sent between devices are 32-bit elements; how exact they have to be, the bound alone decides.
A program may use at most 64 MiB of HBM per device.

v0:
```python
import math

import jax
import jax.numpy as jnp
from jax import lax
from jax.sharding import PartitionSpec as P

fresnel_coef = 0.1
step_size = 4.0
precise = lax.Precision.HIGHEST


def from_behind(array, axis, by):
    count = lax.axis_size(axis)
    pairs = [(i, i + by) for i in range(count) if 0 <= i + by < count]
    return lax.ppermute(array, axis, pairs)


def laplacian(field):
    padded = jnp.pad(field, ((0, 0), (0, 0), (1, 1), (1, 1)))
    return (
        padded[:, :, :-2, 1:-1]
        + padded[:, :, 2:, 1:-1]
        + padded[:, :, 1:-1, :-2]
        + padded[:, :, 1:-1, 2:]
        - 4.0 * field
    )


def propagate(field, sign_value):
    lap_once = laplacian(field)
    lap_twice = laplacian(lap_once)
    damping = 0.5 * fresnel_coef**2
    real_part = field[0] - sign_value * fresnel_coef * lap_once[1] - damping * lap_twice[0]
    imag_part = field[1] + sign_value * fresnel_coef * lap_once[0] - damping * lap_twice[1]
    return jnp.stack([real_part, imag_part])


def times_complex(first_factor, second_factor):
    real_part = first_factor[0] * second_factor[0] - first_factor[1] * second_factor[1]
    imag_part = first_factor[0] * second_factor[1] + first_factor[1] * second_factor[0]
    return jnp.stack([real_part, imag_part])


def conj_times(first_factor, second_factor):
    real_part = first_factor[0] * second_factor[0] + first_factor[1] * second_factor[1]
    imag_part = first_factor[0] * second_factor[1] - first_factor[1] * second_factor[0]
    return jnp.stack([real_part, imag_part])


def left_apply(table, field):
    return jnp.einsum("yk,mkx->myx", table, field, precision=precise)


def right_apply(field, table):
    return jnp.einsum("myk,kx->myx", field, table, precision=precise)


def fourier(field, cosine_table, sine_table):
    half_real = left_apply(cosine_table, field[0]) - left_apply(sine_table, field[1])
    half_imag = left_apply(cosine_table, field[1]) + left_apply(sine_table, field[0])
    full_real = right_apply(half_real, cosine_table) - right_apply(half_imag, sine_table)
    full_imag = right_apply(half_real, sine_table) + right_apply(half_imag, cosine_table)
    return jnp.stack([full_real, full_imag])


def position_terms(
    extended, probe_modes, row_start, col_start, measured_one, cosine_table, sine_table
):
    layers = extended.shape[0]
    pixels = probe_modes.shape[-1]
    window = lax.dynamic_slice(extended, (0, 0, row_start, col_start), (layers, 2, pixels, pixels))
    transmit = window.at[:, 0].add(1.0)
    stored = []
    field_now = probe_modes
    exit_wave = field_now
    for layer_index in range(layers):
        stored.append(field_now)
        exit_wave = times_complex(field_now, transmit[layer_index][:, None])
        if layer_index + 1 < layers:
            field_now = propagate(exit_wave, 1.0)
    far_field = fourier(exit_wave, cosine_table, -sine_table)
    misfit = jnp.sum(far_field[0] ** 2 + far_field[1] ** 2, axis=0) - measured_one
    backward = fourier(2.0 * misfit[None, None] * far_field, cosine_table, sine_table)
    gradients = [None] * layers
    for layer_index in reversed(range(layers)):
        field_now = stored[layer_index]
        grad_term = jnp.sum(conj_times(field_now, backward), axis=1)
        lighting = jnp.sum(field_now[0] ** 2 + field_now[1] ** 2, axis=0)
        gradients[layer_index] = jnp.concatenate([grad_term, lighting[None]], axis=0)
        if layer_index > 0:
            backward = propagate(conj_times(transmit[layer_index][:, None], backward), -1.0)
    return jnp.stack(gradients)


def extend_tile(current, rim_width):
    below_rim = from_behind(current[:, :, :rim_width, :], "tx", -1)
    taller = jnp.concatenate([current, below_rim], axis=2)
    right_rim = from_behind(taller[:, :, :, :rim_width], "ty", -1)
    return jnp.concatenate([taller, right_rim], axis=3)


def return_rims(accumulated, tile_side, rim_width):
    spilled = from_behind(accumulated[:, :, :, tile_side:], "ty", 1)
    narrowed = accumulated[:, :, :, :tile_side].at[:, :, :, :rim_width].add(spilled)
    lower_rim = from_behind(narrowed[:, :, tile_side:, :], "tx", 1)
    return narrowed[:, :, :tile_side, :].at[:, :, :rim_width, :].add(lower_rim)


def on_device(object_slices, probe_modes, corners, measured):
    layers = object_slices.shape[0]
    tile_side = object_slices.shape[2]
    pixels = probe_modes.shape[-1]
    rim_width = pixels // 2
    positions = corners.shape[2]
    share_rows = tile_side // lax.axis_size("scan")
    pixel_index = jnp.arange(pixels, dtype=jnp.int32)
    angles = (pixel_index[:, None] * pixel_index[None, :] % pixels).astype(jnp.float32) * (
        2.0 * math.pi / pixels
    )
    cosine_table = jnp.cos(angles) / math.sqrt(pixels)
    sine_table = jnp.sin(angles) / math.sqrt(pixels)
    current = object_slices
    extended = extend_tile(current, rim_width)

    def visit(position, accumulated):
        row_start = corners[0, 0, position, 0]
        col_start = corners[0, 0, position, 1]
        grad_terms = position_terms(
            extended,
            probe_modes,
            row_start,
            col_start,
            measured[0, 0, position],
            cosine_table,
            sine_table,
        )
        updated = (
            lax.dynamic_slice(accumulated, (0, 0, row_start, col_start), grad_terms.shape)
            + grad_terms
        )
        return lax.dynamic_update_slice(accumulated, updated, (0, 0, row_start, col_start))

    initial = jnp.zeros((layers, 3, tile_side + rim_width, tile_side + rim_width), jnp.float32)
    accumulated = lax.fori_loop(0, positions, visit, initial)
    shared = lax.psum_scatter(
        return_rims(accumulated, tile_side, rim_width), "scan", scatter_dimension=2, tiled=True
    )
    row_first = lax.axis_index("scan") * share_rows
    own_rows = lax.dynamic_slice_in_dim(current, row_first, share_rows, 2)
    own_new = own_rows - step_size * shared[:, :2] / (shared[:, 2:3] + 1.0)
    current = lax.all_gather(own_new, "scan", axis=2, tiled=True)
    return current


def solution(mesh):
    placed = (
        P(None, None, "tx", "ty"),
        P(),
        P("tx", "ty", "scan", None),
        P("tx", "ty", "scan", None, None),
    )
    return jax.shard_map(
        on_device, mesh=mesh, in_specs=placed, out_specs=P(None, None, "tx", "ty"), check_vma=False
    )
```

profile of v0, /device:TPU:0, one launch (start us, length us, event | category | flops | bytes accessed | tf_op | source)
XLA Modules:
  0.0 260.2 jit_solution(9173133318443127020)
XLA Ops:
  10.2 14.2 %collective-permute-done = f32[2,2,128,256]{3,2,1,0:T(8,128)S(1)} collective-permute-done((f32[2,2,128,256]{3,2,1,0:T(8,128)S(1)}, f32[2,2,128,256]{3,2,1,0:T(8,128)S(1)}, u32[]{:S(2)}, u32[]{:S(2)}) %collective-permute-start) | collective-permute-done | bytes 524320 | tf_op jit(solution)/shard_map/ppermute | solution.py:16
  33.8 2.9 %fusion.3 = f32[2,8,256,256]{3,2,1,0:T(8,128)S(1)} fusion(f32[2,8,256,256]{3,2,1,0:T(8,128)S(1)} %pad_maximum_fusion), kind=kLoop, calls=%fused_computation.19 | loop fusion | flops 5242880 | bytes 8388608 | tf_op jit(solution)/shard_map/while/body/eval_jaxpr/sub | solution.py:22
  36.7 2.9 %fusion.7 = f32[2,8,256,256]{3,2,1,0:T(8,128)S(1)} fusion(f32[2,8,256,256]{3,2,1,0:T(8,128)S(1)} %fusion.3), kind=kLoop, calls=%fused_computation.23 | loop fusion | flops 5242880 | bytes 8388608 | tf_op jit(solution)/shard_map/while/body/eval_jaxpr/sub | solution.py:22
  39.7 2.0 add_reduce_fusion
  41.7 4.6 %fusion.79 = f32[8,256,256]{2,1,0:T(8,128)S(1)} fusion(f32[8,256,256]{2,1,0:T(8,128)S(1)} %get-tuple-element.78, f32[8,256,256]{2,1,0:T(8,128)S(1)} %get-tuple-element.77, f32[256,256]{1,0:T(8,128)S(1)} %get-tuple-element.89, f32[256,256]{1,0:T(8,128)S(1)} %get-tuple-element.98), kind=kOutput, calls=%fused_computation.133 | convolution fusion | flops 1613168640 | bytes 6815744 | tf_op jit(solution)/shard_map/while/body/eval_jaxpr/yk,mkx->myx/dot_general | solution.py:52
  46.2 4.6 %fusion.80 = f32[8,256,256]{2,1,0:T(8,128)S(1)} fusion(f32[8,256,256]{2,1,0:T(8,128)S(1)} %get-tuple-element.78, f32[8,256,256]{2,1,0:T(8,128)S(1)} %get-tuple-element.77, f32[256,256]{1,0:T(8,128)S(1)} %get-tuple-element.89, f32[256,256]{1,0:T(8,128)S(1)} %get-tuple-element.98), kind=kOutput, calls=%fused_computation.134 | convolution fusion | flops 1613168640 | bytes 6815744 | tf_op jit(solution)/shard_map/while/body/eval_jaxpr/yk,mkx->myx/dot_general | solution.py:52
  50.8 4.7 %convolution_add_fusion = f32[8,256,256]{2,1,0:T(8,128)S(1)} fusion(f32[8,256,256]{2,1,0:T(8,128)S(1)} %fusion.80, f32[8,256,256]{2,1,0:T(8,128)S(1)} %get-tuple-element.78, f32[8,256,256]{2,1,0:T(8,128)S(1)} %get-tuple-element.77, f32[256,256]{1,0:T(8,128)S(1)} %get-tuple-element.89, f32[256,256]{1,0:T(8,128)S(1)} %get-tuple-element.98), kind=kOutput, calls=%fused_computation.121 | convolution fusion | flops 1613758464 | bytes 8912896 | tf_op jit(solution)/shard_map/while/body/eval_jaxpr/yk,mkx->myx/dot_general | solution.py:52
  55.6 4.5 %fusion.42 = f32[8,256,256]{2,1,0:T(8,128)S(1)} fusion(f32[8,256,256]{2,1,0:T(8,128)S(1)} %convolution_add_fusion), kind=kOutput, calls=%fused_computation.77 | convolution fusion | flops 1611661312 | bytes 4194304 | tf_op jit(solution)/shard_map/while/body/eval_jaxpr/myk,kx->myx/dot_general | solution.py:56
  60.1 4.5 %fusion.40 = f32[8,256,256]{2,1,0:T(8,128)S(1)} fusion(f32[8,256,256]{2,1,0:T(8,128)S(1)} %convolution_add_fusion), kind=kOutput, calls=%fused_computation.75 | convolution fusion | flops 1611595776 | bytes 4194304 | tf_op jit(solution)/shard_map/while/body/eval_jaxpr/myk,kx->myx/dot_general | solution.py:56
  64.6 4.7 %convolution_subtract_fusion = f32[8,256,256]{2,1,0:T(8,128)S(1)} fusion(f32[8,256,256]{2,1,0:T(8,128)S(1)} %fusion.79, f32[8,256,256]{2,1,0:T(8,128)S(1)} %get-tuple-element.78, f32[8,256,256]{2,1,0:T(8,128)S(1)} %get-tuple-element.77, f32[256,256]{1,0:T(8,128)S(1)} %get-tuple-element.89, f32[256,256]{1,0:T(8,128)S(1)} %get-tuple-element.98), kind=kOutput, calls=%fused_computation.122 | convolution fusion | flops 1613758464 | bytes 8912896 | tf_op jit(solution)/shard_map/while/body/eval_jaxpr/yk,mkx->myx/dot_general | solution.py:52
  69.3 4.4 %fusion.62 = f32[8,256,256]{2,1,0:T(8,128)S(1)} fusion(f32[8,256,256]{2,1,0:T(8,128)S(1)} %fusion.42, f32[8,256,256]{2,1,0:T(8,128)S(1)} %convolution_subtract_fusion), kind=kOutput, calls=%fused_computation.117 | convolution fusion | flops 1612120064 | bytes 6291456 | tf_op jit(solution)/shard_map/while/body/eval_jaxpr/myk,kx->myx/dot_general | solution.py:56
  73.7 4.5 %add_reduce_fusion.1 = (f32[256,256]{1,0:T(8,128)S(1)}, f32[8,256,256]{2,1,0:T(8,128)S(1)}) fusion(f32[8,256,256]{2,1,0:T(8,128)S(1)} %fusion.62, f32[8,256,256]{2,1,0:T(8,128)S(1)} %fusion.40, f32[8,256,256]{2,1,0:T(8,128)S(1)} %convolution_subtract_fusion), kind=kOutput, calls=%fused_computation.106 | convolution fusion | flops 1614217216 | bytes 8650752 | tf_op jit(solution)/shard_map/while/body/eval_jaxpr/myk,kx->myx/dot_general | solution.py:56
  79.0 4.3 %fusion.57 = f32[8,256,256]{2,1,0:T(8,128)S(1)} fusion(f32[2,8,256,256]{3,2,1,0:T(8,128)S(1)} %maximum_multiply_fusion), kind=kOutput, calls=%fused_computation.112 | convolution fusion | flops 1611595776 | bytes 4194304 | tf_op jit(solution)/shard_map/while/body/eval_jaxpr/yk,mkx->myx/dot_general | solution.py:52
  83.3 4.3 %fusion.56 = f32[8,256,256]{2,1,0:T(8,128)S(1)} fusion(f32[2,8,256,256]{3,2,1,0:T(8,128)S(1)} %maximum_multiply_fusion), kind=kOutput, calls=%fused_computation.111 | convolution fusion | flops 1611595776 | bytes 4194304 | tf_op jit(solution)/shard_map/while/body/eval_jaxpr/yk,mkx->myx/dot_general | solution.py:52
  87.6 4.4 %fusion.61 = f32[8,256,256]{2,1,0:T(8,128)S(1)} fusion(f32[8,256,256]{2,1,0:T(8,128)S(1)} %fusion.56, f32[2,8,256,256]{3,2,1,0:T(8,128)S(1)} %maximum_multiply_fusion), kind=kOutput, calls=%fused_computation.116 | convolution fusion | flops 1612120064 | bytes 6291456 | tf_op jit(solution)/shard_map/while/body/eval_jaxpr/yk,mkx->myx/dot_general | solution.py:52
  92.0 4.3 %fusion.34 = f32[8,256,256]{2,1,0:T(8,128)S(1)} fusion(f32[8,256,256]{2,1,0:T(8,128)S(1)} %fusion.61), kind=kOutput, calls=%fused_computation.69 | convolution fusion | flops 1611595776 | bytes 4194304 | tf_op jit(solution)/shard_map/while/body/eval_jaxpr/myk,kx->myx/dot_general | solution.py:56
  96.3 4.3 %fusion.32 = f32[8,256,256]{2,1,0:T(8,128)S(1)} fusion(f32[8,256,256]{2,1,0:T(8,128)S(1)} %fusion.61), kind=kOutput, calls=%fused_computation.67 | convolution fusion | flops 1611595776 | bytes 4194304 | tf_op jit(solution)/shard_map/while/body/eval_jaxpr/myk,kx->myx/dot_general | solution.py:56
  100.7 4.5 %fusion.60 = f32[8,256,256]{2,1,0:T(8,128)S(1)} fusion(f32[8,256,256]{2,1,0:T(8,128)S(1)} %fusion.57, f32[2,8,256,256]{3,2,1,0:T(8,128)S(1)} %maximum_multiply_fusion), kind=kOutput, calls=%fused_computation.115 | convolution fusion | flops 1612120064 | bytes 6291456 | tf_op jit(solution)/shard_map/while/body/eval_jaxpr/yk,mkx->myx/dot_general | solution.py:52
  105.2 4.4 %fusion.68 = f32[8,256,256]{2,1,0:T(8,128)S(1)} fusion(f32[8,256,256]{2,1,0:T(8,128)S(1)} %fusion.34, f32[8,256,256]{2,1,0:T(8,128)S(1)} %fusion.60), kind=kOutput, calls=%fused_computation.119 | convolution fusion | flops 1612120064 | bytes 6291456 | tf_op jit(solution)/shard_map/while/body/eval_jaxpr/myk,kx->myx/dot_general | solution.py:56
  109.6 4.5 %fusion.71 = f32[8,256,256]{2,1,0:T(8,128)S(1)} fusion(f32[8,256,256]{2,1,0:T(8,128)S(1)} %fusion.32, f32[8,256,256]{2,1,0:T(8,128)S(1)} %fusion.60), kind=kOutput, calls=%fused_computation.120 | convolution fusion | flops 1612120064 | bytes 6291456 | tf_op jit(solution)/shard_map/while/body/eval_jaxpr/myk,kx->myx/dot_general | solution.py:56
  114.9 3.2 %fusion.11 = f32[2,8,256,256]{3,2,1,0:T(8,128)S(1)} fusion(f32[2,8,256,256]{3,2,1,0:T(8,128)S(1)} %pad_maximum_fusion.1), kind=kLoop, calls=%fused_computation.27 | loop fusion | flops 5242880 | bytes 8388608 | tf_op jit(solution)/shard_map/while/body/eval_jaxpr/sub | solution.py:22
  118.1 2.9 %fusion.15 = f32[2,8,256,256]{3,2,1,0:T(8,128)S(1)} fusion(f32[2,8,256,256]{3,2,1,0:T(8,128)S(1)} %fusion.11), kind=kLoop, calls=%fused_computation.31 | loop fusion | flops 5242880 | bytes 8388608 | tf_op jit(solution)/shard_map/while/body/eval_jaxpr/sub | solution.py:22
  121.0 5.0 %fusion.51 = (f32[1,8,256,256]{3,2,1,0:T(8,128)}, f32[8,256,256]{2,1,0:T(8,128)}, f32[8,256,256]{2,1,0:T(8,128)}, f32[1,8,256,256]{3,2,1,0:T(8,128)}, f32[1,8,256,256]{3,2,1,0:T(8,128)}) fusion(f32[2,8,256,256]{3,2,1,0:T(8,128)S(1)} %copy-done, f32[2,8,256,256]{3,2,1,0:T(8,128)S(1)} %fusion.15, f32[2,8,256,256]{3,2,1,0:T(8,128)S(1)} %fusion.11, ...), kind=kLoop, calls=%fused_computation.91 | loop fusion | flops 12058624 | bytes 31981568 | tf_op jit(solution)/shard_map/while/body/eval_jaxpr/stack | solution.py:48
  126.0 3.1 %fusion.53 = (f32[1,8,256,256]{3,2,1,0:T(8,128)S(1)}, f32[256,256]{1,0:T(8,128)S(1)}) fusion(f32[8,256,256]{2,1,0:T(8,128)} %get-tuple-element.75, f32[8,256,256]{2,1,0:T(8,128)} %get-tuple-element.74, f32[2,8,256,256]{3,2,1,0:T(8,128)S(1)} %copy-done), kind=kLoop, calls=%fused_computation.93 | loop fusion | flops 3604480 | bytes 10747904 | tf_op jit(solution)/shard_map/while/body/eval_jaxpr/stack | solution.py:48
  133.2 19.9 %dynamic_update_slice.4 = f32[2,3,384,384]{3,2,1,0:T(8,128)S(1)} dynamic-update-slice(f32[2,3,384,384]{3,2,1,0:T(8,128)S(1)} %broadcast_in_dim.15, f32[2,3,256,256]{3,2,1,0:T(8,128)} %pad_maximum_fusion.2, s32[]{:T(128)} %constant.153.clone.1, s32[]{:T(128)} %constant.153.clone.1, s32[]{:T(128)S(6)} %select_n.61, s32[]{:T(128)S(6)} %select_n.63) | dynamic-update-slice | bytes 3145732 | tf_op jit(solution)/shard_map/while/body/eval_jaxpr/dynamic_update_slice | solution.py:142
  153.2 5.2 %collective-permute-start.2 = (f32[2,3,384,128]{3,2,1,0:T(8,128)S(1)}, f32[2,3,384,128]{3,2,1,0:T(8,128)S(1)}, u32[]{:S(2)}, u32[]{:S(2)}) collective-permute-start(f32[2,3,384,128]{3,2,1,0:T(8,128)S(1)} %slice.340), channel_id=1, source_target_pairs={{0,1},{2,3},{4,5},{6,7},{8,9},{10,11},{12,13},{14,15},{16,17},{18,... | collective-permute-start | bytes 3538952 | tf_op jit(solution)/shard_map/ppermute | solution.py:16
  158.6 2.2 collective-permute-done.2
  161.0 4.9 %collective-permute-start.3 = (f32[2,3,128,256]{3,2,1,0:T(8,128)S(1)}, f32[2,3,128,256]{3,2,1,0:T(8,128)S(1)}, u32[]{:S(2)}, u32[]{:S(2)}) collective-permute-start(f32[2,3,128,256]{3,2,1,0:T(8,128)S(1)} %slice.343), channel_id=1, source_target_pairs={{0,2},{2,4},{4,6},{1,3},{3,5},{5,7},{8,10},{10,12},{12,14},{9,11},... | collective-permute-start | bytes 2359304 | tf_op jit(solution)/shard_map/ppermute | solution.py:16
  166.0 17.2 %collective-permute-done.3 = f32[2,3,128,256]{3,2,1,0:T(8,128)S(1)} collective-permute-done((f32[2,3,128,256]{3,2,1,0:T(8,128)S(1)}, f32[2,3,128,256]{3,2,1,0:T(8,128)S(1)}, u32[]{:S(2)}, u32[]{:S(2)}) %collective-permute-start.3) | collective-permute-done | bytes 786464 | tf_op jit(solution)/shard_map/ppermute | solution.py:16
  184.5 36.3 %reduce-scatter.2.cloned.1.call-done = f32[2,3,64,256]{3,2,1,0:T(8,128)} async-done(((f32[2,3,256,256]{3,2,1,0:T(8,128)}), f32[2,3,64,256]{3,2,1,0:T(8,128)}) %reduce-scatter.2.cloned.1.call-update) | async-done | bytes 393232 | tf_op jit(solution)/shard_map/reduce_scatter | solution.py:146
  223.6 27.0 %all-gather.2.cloned.1.call-done = f32[2,2,256,256]{3,2,1,0:T(8,128)} async-done(((f32[2,2,64,256]{3,2,1,0:T(8,128)}), f32[2,2,256,256]{3,2,1,0:T(8,128)}) %all-gather.2.cloned.1.call-update) | async-done | bytes 1048592 | tf_op jit(solution)/shard_map/all_gather | solution.py:152
  250.6 2.3 copy.42
  (49 shorter events, 19.6 us)
Async XLA Ops:
  6.5 214.3 %reduce-scatter.2.cloned.1.call-start = ((), (), s32[]{:S(2)}) async-start(), calls=%async_computation.1 | async-start | bytes 1966080 | tf_op jit(solution)/shard_map/reduce_scatter | solution.py:146
  7.6 18.2 %copy-start.6 = (s32[1,1,1,2]{3,2,1,0:T(1,128)S(1)}, s32[1,1,1,2]{3,2,1,0:T(1,128)}, u32[]{:S(2)}) copy-start(s32[1,1,1,2]{3,2,1,0:T(1,128)} %param.12) | copy-start | bytes 28
  7.6 16.8 %collective-permute-start = (f32[2,2,128,256]{3,2,1,0:T(8,128)S(1)}, f32[2,2,128,256]{3,2,1,0:T(8,128)S(1)}, u32[]{:S(2)}, u32[]{:S(2)}) collective-permute-start(f32[2,2,128,256]{3,2,1,0:T(8,128)S(1)} %slice.282), channel_id=1, source_target_pairs={{2,0},{4,2},{6,4},{3,1},{5,3},{7,5},{10,8},{12,10},{14,12},{11,9},... | collective-permute-start | bytes 1572872 | tf_op jit(solution)/shard_map/ppermute | solution.py:16
  24.5 5.5 %collective-permute-start.1 = (f32[2,2,384,128]{3,2,1,0:T(8,128)S(1)}, f32[2,2,384,128]{3,2,1,0:T(8,128)S(1)}, u32[]{:S(2)}, u32[]{:S(2)}) collective-permute-start(f32[2,2,384,128]{3,2,1,0:T(8,128)S(1)} %slice.323), channel_id=1, source_target_pairs={{1,0},{3,2},{5,4},{7,6},{9,8},{11,10},{13,12},{15,14},{17,16},{19,... | collective-permute-start | bytes 2359304 | tf_op jit(solution)/shard_map/ppermute | solution.py:16
  30.7 2.2 copy-start
  73.7 4.5 %copy-start.5 = (f32[1,1,1,256,256]{4,3,2,1,0:T(8,128)S(1)}, f32[1,1,1,256,256]{4,3,2,1,0:T(8,128)}, u32[]{:S(2)}) copy-start(f32[1,1,1,256,256]{4,3,2,1,0:T(8,128)} %param.13) | copy-start | bytes 786436
  126.0 3.1 %copy-start.3 = (f32[1,8,256,256]{3,2,1,0:T(8,128)S(1)}, f32[1,8,256,256]{3,2,1,0:T(8,128)}, u32[]{:S(2)}) copy-start(f32[1,8,256,256]{3,2,1,0:T(8,128)} %get-tuple-element.73) | copy-start | bytes 6291460
  129.1 1.6 copy-start.1
  129.1 2.2 copy-start.2
  153.2 7.6 %collective-permute-start.2 = (f32[2,3,384,128]{3,2,1,0:T(8,128)S(1)}, f32[2,3,384,128]{3,2,1,0:T(8,128)S(1)}, u32[]{:S(2)}, u32[]{:S(2)}) collective-permute-start(f32[2,3,384,128]{3,2,1,0:T(8,128)S(1)} %slice.340), channel_id=1, source_target_pairs={{0,1},{2,3},{4,5},{6,7},{8,9},{10,11},{12,13},{14,15},{16,17},{18,... | collective-permute-start | bytes 3538952 | tf_op jit(solution)/shard_map/ppermute | solution.py:16
  161.0 22.2 %collective-permute-start.3 = (f32[2,3,128,256]{3,2,1,0:T(8,128)S(1)}, f32[2,3,128,256]{3,2,1,0:T(8,128)S(1)}, u32[]{:S(2)}, u32[]{:S(2)}) collective-permute-start(f32[2,3,128,256]{3,2,1,0:T(8,128)S(1)} %slice.343), channel_id=1, source_target_pairs={{0,2},{2,4},{4,6},{1,3},{3,5},{5,7},{8,10},{10,12},{12,14},{9,11},... | collective-permute-start | bytes 2359304 | tf_op jit(solution)/shard_map/ppermute | solution.py:16
  183.3 1.1 copy-start.4
  184.5 66.1 %all-gather.2.cloned.1.call-start = ((), (), s32[]{:S(2)}) async-start(), calls=%async_computation.2 | async-start | bytes 1310720 | tf_op jit(solution)/shard_map/all_gather | solution.py:152
Sparse Core Ops, SparseCore 0:
  184.6 36.2 reduce-scatter.1
  223.7 26.8 all-gather.1
where the time goes:
time: 265 us; the launch traced here: 260 us
  waiting for transfers between devices  96.9 us (37%)
  matrix products  71.5 us (27%)
  local copies, waits for them, and re-layouts  30.7 us (12%)
  other arithmetic  30.4 us (11%)
  between operations  17.9 us (7%)
  starting transfers between devices  12.7 us (5%)
    reduce_scatter x1, waiting for transfers between devices, on_device(): lax.psum_scatter(return_rims(accumulated, tile_side, rim_width), 'scan',...  36.3 us
    dot_general x8, matrix products, left_apply(): return jnp.einsum('yk,mkx->myx', table, field, precision=precise)  36.1 us
    dot_general x8, matrix products, right_apply(): return jnp.einsum('myk,kx->myx', field, table, precision=precise)  35.4 us
    ppermute x4, waiting for transfers between devices, from_behind(): return lax.ppermute(array, axis, pairs)  33.5 us
    all_gather x1, waiting for transfers between devices, on_device(): current = lax.all_gather(own_new, 'scan', axis=2, tiled=True)  27 us
    dynamic_update_slice x1, local copies, waits for them, and re-layouts, visit(): lax.dynamic_update_slice(accumulated, updated, (0, 0, row_start, col_start))  19.9 us
    ppermute x4, starting transfers between devices, from_behind(): return lax.ppermute(array, axis, pairs)  12.7 us
    sub x4, other arithmetic, laplacian(): padded[:, :, :-2, 1:-1] + padded[:, :, 2:, 1:-1] + padded[:, :, 1:-1, :-2]  11.9 us
  transfers between devices with their start and end apart: 6, of which 5 were waited for; matrix products, arithmetic and copies ran while one was open for 1% of the time, Pallas kernels for 0%

commit v1 on v0

v1 whole, which is shorter than its diff:
```python
import functools
import math

import jax
import jax.numpy as jnp
import numpy as np
from jax import lax
from jax.experimental import pallas as pl
from jax.experimental.pallas import tpu as pltpu
from jax.sharding import PartitionSpec as P

fresnel_coef = 0.1
step_size = 4.0
damping = 0.5 * fresnel_coef**2


def dft_tables(pixels):
    half = pixels // 2
    tables = []
    for parity in range(2):
        freq = 2 * np.arange(half) + parity
        angle = 2.0 * np.pi * ((freq[:, None] * np.arange(half)[None, :]) % pixels) / pixels
        c, s = np.cos(angle) / math.sqrt(pixels), np.sin(angle) / math.sqrt(pixels)
        tables.append(np.block([[c, s], [-s, c]]))
    tables += [t.T for t in tables]
    out = []
    for t in tables:
        t32 = t.astype(np.float32)
        high = t32.astype(jnp.bfloat16)
        low = (t - high.astype(np.float64)).astype(np.float32).astype(jnp.bfloat16)
        out += [high, low]
    return np.stack(out)


def split2(x):
    high = x.astype(jnp.bfloat16)
    return high, (x - high.astype(jnp.float32)).astype(jnp.bfloat16)


def right_dot(x, high, low):
    xh, xl = split2(x)
    lhs = jnp.concatenate([xh, xl, xh], axis=1)
    rhs = jnp.concatenate([high, high, low], axis=0)
    return jnp.dot(lhs, rhs, preferred_element_type=jnp.float32)


def left_dot(high, low, x):
    xh, xl = split2(x)
    lhs = jnp.concatenate([high, high, low], axis=1)
    rhs = jnp.concatenate([xh, xl, xh], axis=0)
    return jnp.dot(lhs, rhs, preferred_element_type=jnp.float32)


def propagate(re, im, sign, edges):
    first_row, last_row, first_col, last_col = edges
    n = re.shape[0]

    def lap(v):
        up = jnp.where(first_row, 0.0, pltpu.roll(v, 1, 0))
        down = jnp.where(last_row, 0.0, pltpu.roll(v, n - 1, 0))
        left = jnp.where(first_col, 0.0, pltpu.roll(v, 1, 1))
        right = jnp.where(last_col, 0.0, pltpu.roll(v, n - 1, 1))
        return (up + down) + (left + right) - 4.0 * v

    l_re, l_im = lap(re), lap(im)
    ll_re, ll_im = lap(l_re), lap(l_im)
    coef = sign * fresnel_coef
    return re - coef * l_im - damping * ll_re, im + coef * l_re - damping * ll_im


def position_kernel(
    corner, ext, probe, measured, tables, acc, trans, wave1, far, misfit, sums, padded
):
    modes, n = probe.shape[1], probe.shape[2]
    h = n // 2
    r, c = corner[0], corner[1]
    wide = ext.shape[2]
    up, left = jnp.where(r == 0, 0, wide - r), jnp.where(c == 0, 0, wide - c)
    for p in range(4):
        rows = pltpu.roll(ext[p], up, 0)[:n]
        window = pltpu.roll(rows, left, 1)[:, :n]
        trans[p] = window + 1.0 if p % 2 == 0 else window
    row = lax.broadcasted_iota(jnp.int32, (n, n), 0)
    col = lax.broadcasted_iota(jnp.int32, (n, n), 1)
    edges = (row == 0, row == n - 1, col == 0, col == n - 1)
    one_hot = jnp.where(col == jnp.where(row < h, 2 * row, 2 * (row - h) + 1), 1.0, 0.0)
    one_hot_t = jnp.where(row == jnp.where(col < h, 2 * col, 2 * (col - h) + 1), 1.0, 0.0)

    def three(x):
        hi, rest = split2(x)
        mid = rest
        lo = (x - hi.astype(jnp.float32) - mid.astype(jnp.float32)).astype(jnp.bfloat16)
        return hi, mid, lo

    ph, pt = one_hot.astype(jnp.bfloat16), one_hot_t.astype(jnp.bfloat16)
    half_done = sum(
        jnp.dot(ph, part, preferred_element_type=jnp.float32) for part in three(measured[...])
    )
    misfit[...] = -sum(
        jnp.dot(part, pt, preferred_element_type=jnp.float32) for part in three(half_done)
    )
    sums[...] = jnp.zeros_like(sums)

    def forward(m, _):
        re0, im0 = probe[0, m], probe[1, m]
        sums[2] += re0 * re0 + im0 * im0
        tr, ti = trans[0], trans[1]
        re1, im1 = propagate(re0 * tr - im0 * ti, re0 * ti + im0 * tr, 1.0, edges)
        wave1[0, m] = re1
        wave1[1, m] = im1
        sums[5] += re1 * re1 + im1 * im1
        tr, ti = trans[2], trans[3]
        er, ei = re1 * tr - im1 * ti, re1 * ti + im1 * tr
        even = right_dot(
            jnp.concatenate([er[:, :h] + er[:, h:], ei[:, :h] + ei[:, h:]], axis=1),
            tables[4], tables[5],
        )
        odd = right_dot(
            jnp.concatenate([er[:, :h] - er[:, h:], ei[:, :h] - ei[:, h:]], axis=1),
            tables[6], tables[7],
        )
        fr = jnp.concatenate([even[:, :h], odd[:, :h]], axis=1)
        fi = jnp.concatenate([even[:, h:], odd[:, h:]], axis=1)
        f_even = left_dot(
            tables[0], tables[1],
            jnp.concatenate([fr[:h] + fr[h:], fi[:h] + fi[h:]], axis=0),
        )
        f_odd = left_dot(
            tables[2], tables[3],
            jnp.concatenate([fr[:h] - fr[h:], fi[:h] - fi[h:]], axis=0),
        )
        far[0, m] = f_even
        far[1, m] = f_odd
        misfit[:h] += f_even[:h] * f_even[:h] + f_even[h:] * f_even[h:]
        misfit[h:] += f_odd[:h] * f_odd[:h] + f_odd[h:] * f_odd[h:]
        return 0

    lax.fori_loop(0, modes, forward, 0)

    def backward(m, _):
        m_even, m_odd = 2.0 * misfit[:h], 2.0 * misfit[h:]
        b_even = left_dot(
            tables[4], tables[5], far[0, m] * jnp.concatenate([m_even, m_even], axis=0)
        )
        b_odd = left_dot(
            tables[6], tables[7], far[1, m] * jnp.concatenate([m_odd, m_odd], axis=0)
        )
        top, low = b_even + b_odd, b_even - b_odd
        br = jnp.concatenate([top[:h], low[:h]], axis=0)
        bi = jnp.concatenate([top[h:], low[h:]], axis=0)
        c_even = right_dot(
            jnp.concatenate([br[:, :h], bi[:, :h]], axis=1), tables[0], tables[1]
        )
        c_odd = right_dot(
            jnp.concatenate([br[:, h:], bi[:, h:]], axis=1), tables[2], tables[3]
        )
        lo, hi = c_even + c_odd, c_even - c_odd
        br = jnp.concatenate([lo[:, :h], hi[:, :h]], axis=1)
        bi = jnp.concatenate([lo[:, h:], hi[:, h:]], axis=1)
        wr, wi = wave1[0, m], wave1[1, m]
        sums[3] += wr * br + wi * bi
        sums[4] += wr * bi - wi * br
        tr, ti = trans[2], trans[3]
        br, bi = propagate(tr * br + ti * bi, tr * bi - ti * br, -1.0, edges)
        wr, wi = probe[0, m], probe[1, m]
        sums[0] += wr * br + wi * bi
        sums[1] += wr * bi - wi * br
        return 0

    lax.fori_loop(0, modes, backward, 0)
    padded[...] = jnp.zeros_like(padded)
    for p in range(6):
        padded[:n, :n] = sums[p]
        acc[p] = pltpu.roll(pltpu.roll(padded[...], r, 0), c, 1)


def position_terms(corner, extended, probe_modes, measured_one, tables):
    layers, n = extended.shape[0], probe_modes.shape[-1]
    modes = probe_modes.shape[1]
    wide = extended.shape[-1]
    vmem = pl.BlockSpec(memory_space=pltpu.VMEM)
    return pl.pallas_call(
        position_kernel,
        out_shape=jax.ShapeDtypeStruct((6, wide, wide), jnp.float32),
        in_specs=[pl.BlockSpec(memory_space=pltpu.SMEM)] + [vmem] * 4,
        out_specs=vmem,
        scratch_shapes=[
            pltpu.VMEM((4, n, n), jnp.float32),
            pltpu.VMEM((2, modes, n, n), jnp.float32),
            pltpu.VMEM((2, modes, n, n), jnp.float32),
            pltpu.VMEM((n, n), jnp.float32),
            pltpu.VMEM((6, n, n), jnp.float32),
            pltpu.VMEM((wide, wide), jnp.float32),
        ],
        compiler_params=pltpu.CompilerParams(vmem_limit_bytes=60 * 1024 * 1024),
        name="position_terms",
    )(corner, extended, probe_modes, measured_one, tables)


def from_behind(array, axis, by):
    count = lax.axis_size(axis)
    pairs = [(i, i + by) for i in range(count) if 0 <= i + by < count]
    return lax.ppermute(array, axis, pairs)


def extend_tile(current, rim_width):
    below_rim = from_behind(current[:, :, :rim_width, :], "tx", -1)
    taller = jnp.concatenate([current, below_rim], axis=2)
    right_rim = from_behind(taller[:, :, :, :rim_width], "ty", -1)
    return jnp.concatenate([taller, right_rim], axis=3)


def return_rims(accumulated, tile_side, rim_width):
    spilled = from_behind(accumulated[:, :, :, tile_side:], "ty", 1)
    narrowed = accumulated[:, :, :, :tile_side].at[:, :, :, :rim_width].add(spilled)
    lower_rim = from_behind(narrowed[:, :, tile_side:, :], "tx", 1)
    return narrowed[:, :, :tile_side, :].at[:, :, :rim_width, :].add(lower_rim)


def on_device(object_slices, probe_modes, corners, measured):
    layers = object_slices.shape[0]
    tile_side = object_slices.shape[2]
    pixels = probe_modes.shape[-1]
    rim_width = pixels // 2
    positions = corners.shape[2]
    share_rows = tile_side // lax.axis_size("scan")
    wide = tile_side + rim_width
    tables = jnp.asarray(dft_tables(pixels))
    current = object_slices
    extended = extend_tile(current, rim_width).reshape(2 * layers, wide, wide)
    accumulated = sum(
        position_terms(
            corners[0, 0, position], extended, probe_modes, measured[0, 0, position], tables
        )
        for position in range(positions)
    ).reshape(layers, 3, wide, wide)
    shared = lax.psum_scatter(
        return_rims(accumulated, tile_side, rim_width), "scan", scatter_dimension=2, tiled=True
    )
    row_first = lax.axis_index("scan") * share_rows
    own_rows = lax.dynamic_slice_in_dim(current, row_first, share_rows, 2)
    own_new = own_rows - step_size * shared[:, :2] / (shared[:, 2:3] + 1.0)
    return lax.all_gather(own_new, "scan", axis=2, tiled=True)


def solution(mesh):
    placed = (
        P(None, None, "tx", "ty"),
        P(),
        P("tx", "ty", "scan", None),
        P("tx", "ty", "scan", None, None),
    )
    return jax.shard_map(
        on_device, mesh=mesh, in_specs=placed, out_specs=P(None, None, "tx", "ty"), check_vma=False
    )
```

time: 265 us -> 167 us (0.63)
  the two profiles are of different devices: /device:TPU:0 before, /device:TPU:13 now
where the time goes in v1:
time: 167 us; the launch traced here: 164 us
  waiting for transfers between devices  96.9 us (58%)
  Pallas kernels  30.2 us (18%)
  between operations  13.5 us (8%)
  starting transfers between devices  9.8 us (6%)
  local copies, waits for them, and re-layouts  8.07 us (5%)
  other arithmetic  5.71 us (3%)
    ppermute x4, waiting for transfers between devices, from_behind(): return lax.ppermute(array, axis, pairs)  34.7 us
    reduce_scatter x1, waiting for transfers between devices, on_device(): lax.psum_scatter(return_rims(accumulated, tile_side, rim_width), 'scan',...  33.9 us
    pallas_call x1, Pallas kernels, position_terms(): pl.pallas_call(position_kernel, out_shape=jax.ShapeDtypeStruct((6, wide,...  30.2 us
    all_gather x1, waiting for transfers between devices, on_device(): return lax.all_gather(own_new, 'scan', axis=2, tiled=True)  28.3 us
    ppermute x4, starting transfers between devices, from_behind(): return lax.ppermute(array, axis, pairs)  9.76 us
    unnamed x6, local copies, waits for them, and re-layouts  3.5 us
  transfers between devices with their start and end apart: 6, of which 6 were waited for; matrix products, arithmetic and copies ran while one was open for 1% of the time, Pallas kernels for 0%

profile of v1, /device:TPU:13, one launch (start us, length us, event | category | flops | bytes accessed | tf_op | source)
XLA Modules:
  0.0 164.3 jit_solution(12288751749008401041)
XLA Ops:
  6.5 0.0 copy-start.1
  6.5 0.0 reduce-scatter.2.cloned.1.call-start
  6.5 1.2 slice.84
  7.7 3.1 %collective-permute-start = (f32[2,2,128,256]{3,2,1,0:T(8,128)S(1)}, f32[2,2,128,256]{3,2,1,0:T(8,128)S(1)}, u32[]{:S(2)}, u32[]{:S(2)}) collective-permute-start(f32[2,2,128,256]{3,2,1,0:T(8,128)S(1)} %slice.84), channel_id=1, source_target_pairs={{2,0},{4,2},{6,4},{3,1},{5,3},{7,5},{10,8},{12,10},{14,12},{11,9},... | collective-permute-start | bytes 1572872 | tf_op jit(solution)/shard_map/ppermute | solution.py:203
  10.8 0.0 copy-done.1
  10.8 0.1 constant_dynamic-update-slice_fusion.1
  10.9 11.5 %collective-permute-done = f32[2,2,128,256]{3,2,1,0:T(8,128)S(1)} collective-permute-done((f32[2,2,128,256]{3,2,1,0:T(8,128)S(1)}, f32[2,2,128,256]{3,2,1,0:T(8,128)S(1)}, u32[]{:S(2)}, u32[]{:S(2)}) %collective-permute-start) | collective-permute-done | bytes 524320 | tf_op jit(solution)/shard_map/ppermute | solution.py:203
  22.4 0.1 slice.94
  22.5 3.5 %collective-permute-start.1 = (f32[2,2,384,128]{3,2,1,0:T(8,128)S(1)}, f32[2,2,384,128]{3,2,1,0:T(8,128)S(1)}, u32[]{:S(2)}, u32[]{:S(2)}) collective-permute-start(f32[2,2,384,128]{3,2,1,0:T(8,128)S(1)} %slice.94), channel_id=1, source_target_pairs={{1,0},{3,2},{5,4},{7,6},{9,8},{11,10},{13,12},{15,14},{17,16},{19,... | collective-permute-start | bytes 2359304 | tf_op jit(solution)/shard_map/ppermute | solution.py:203
  26.0 1.8 %collective-permute-done.1 = f32[2,2,384,128]{3,2,1,0:T(8,128)S(1)} collective-permute-done((f32[2,2,384,128]{3,2,1,0:T(8,128)S(1)}, f32[2,2,384,128]{3,2,1,0:T(8,128)S(1)}, u32[]{:S(2)}, u32[]{:S(2)}) %collective-permute-start.1) | collective-permute-done | bytes 786464 | tf_op jit(solution)/shard_map/ppermute | solution.py:203
  27.8 1.6 pad_maximum_fusion
  29.4 30.2 %position_terms.1 = f32[6,384,384]{2,1,0:T(8,128)} custom-call(s32[2]{0:T(128)} %bitcast.11, f32[4,384,384]{2,1,0:T(8,128)} %bitcast.9, f32[2,8,256,256]{3,2,1,0:T(8,128)} %probe.1, f32[256,256]{1,0:T(8,128)} %bitcast.10, bf16[8,256,256]{2,1,0:T(8,128)(2,1)} %constant.68.clone.tables), custom_call_target="tpu_custom_call" | custom-call | tf_op jit(solution)/shard_map/position_terms/pallas_call | solution.py:182
  59.7 1.3 slice.97
  61.0 1.3 collective-permute-start.2
  62.3 1.8 %slice.95 = f32[2,3,384,256]{3,2,1,0:T(8,128)S(1)} slice(f32[2,3,384,384]{3,2,1,0:T(8,128)} %bitcast.7), slice={[0:2], [0:3], [0:384], [0:256]} | slice | bytes 4718592 | tf_op jit(solution)/shard_map/slice | solution.py:215
  64.1 1.6 collective-permute-done.2
  65.8 1.4 fusion
  67.2 0.1 slice.100
  67.2 1.9 %collective-permute-start.3 = (f32[2,3,128,256]{3,2,1,0:T(8,128)S(1)}, f32[2,3,128,256]{3,2,1,0:T(8,128)S(1)}, u32[]{:S(2)}, u32[]{:S(2)}) collective-permute-start(f32[2,3,128,256]{3,2,1,0:T(8,128)S(1)} %slice.100), channel_id=1, source_target_pairs={{0,2},{2,4},{4,6},{1,3},{3,5},{5,7},{8,10},{10,12},{12,14},{9,11},... | collective-permute-start | bytes 2359304 | tf_op jit(solution)/shard_map/ppermute | solution.py:203
  69.2 0.1 slice.98
  69.3 19.7 %collective-permute-done.3 = f32[2,3,128,256]{3,2,1,0:T(8,128)S(1)} collective-permute-done((f32[2,3,128,256]{3,2,1,0:T(8,128)S(1)}, f32[2,3,128,256]{3,2,1,0:T(8,128)S(1)}, u32[]{:S(2)}, u32[]{:S(2)}) %collective-permute-start.3) | collective-permute-done | bytes 786464 | tf_op jit(solution)/shard_map/ppermute | solution.py:203
  89.0 0.1 fusion.1
  89.1 0.0 copy-start
  89.1 1.1 copy-done
  90.2 0.0 reduce-scatter.2.cloned.1.call-update
  90.3 0.0 all-gather.2.cloned.1.call-start
  90.3 33.9 %reduce-scatter.2.cloned.1.call-done = f32[2,3,64,256]{3,2,1,0:T(8,128)} async-done(((f32[2,3,256,256]{3,2,1,0:T(8,128)}), f32[2,3,64,256]{3,2,1,0:T(8,128)}) %reduce-scatter.2.cloned.1.call-update) | async-done | bytes 393232 | tf_op jit(solution)/shard_map/reduce_scatter | solution.py:237
  124.2 0.9 fusion.4
  125.1 1.7 %fusion.3 = f32[2,2,64,256]{3,2,1,0:T(8,128)} fusion(f32[2,3,64,256]{3,2,1,0:T(8,128)} %reduce-scatter.2.cloned.1.call-done, f32[2,2,256,256]{3,2,1,0:T(8,128)S(1)} %copy-done.1, s32[]{:T(128)S(6)} %select_n.3, f32[2,64,256]{2,1,0:T(8,128)S(1)} %fusion.4), kind=kLoop, calls=%fused_computation.7 | loop fusion | flops 196608 | bytes 917508 | tf_op jit(solution)/shard_map/sub | solution.py:242
  126.9 0.0 all-gather.2.cloned.1.call-update
  126.9 28.3 %all-gather.2.cloned.1.call-done = f32[2,2,256,256]{3,2,1,0:T(8,128)} async-done(((f32[2,2,64,256]{3,2,1,0:T(8,128)}), f32[2,2,256,256]{3,2,1,0:T(8,128)}) %all-gather.2.cloned.1.call-update) | async-done | bytes 1048592 | tf_op jit(solution)/shard_map/all_gather | solution.py:243
  155.1 2.3 %copy.10 = f32[2,2,256,256]{3,2,1,0:T(8,128)} copy(f32[2,2,256,256]{3,2,1,0:T(8,128)} %all-gather.2.cloned.1.call-done) | data formatting | bytes 2097152
  (1 shorter events, 0.0 us)
Async XLA Ops:
  6.5 4.2 %copy-start.1 = (f32[2,2,256,256]{3,2,1,0:T(8,128)S(1)}, f32[2,2,256,256]{3,2,1,0:T(8,128)}, u32[]{:S(2)}) copy-start(f32[2,2,256,256]{3,2,1,0:T(8,128)} %param.9) | copy-start | bytes 3145732
  6.5 117.7 %reduce-scatter.2.cloned.1.call-start = ((), (), s32[]{:S(2)}) async-start(), calls=%async_computation.1 | async-start | bytes 1966080 | tf_op jit(solution)/shard_map/reduce_scatter | solution.py:237
  7.7 14.7 %collective-permute-start = (f32[2,2,128,256]{3,2,1,0:T(8,128)S(1)}, f32[2,2,128,256]{3,2,1,0:T(8,128)S(1)}, u32[]{:S(2)}, u32[]{:S(2)}) collective-permute-start(f32[2,2,128,256]{3,2,1,0:T(8,128)S(1)} %slice.84), channel_id=1, source_target_pairs={{2,0},{4,2},{6,4},{3,1},{5,3},{7,5},{10,8},{12,10},{14,12},{11,9},... | collective-permute-start | bytes 1572872 | tf_op jit(solution)/shard_map/ppermute | solution.py:203
  22.5 5.3 %collective-permute-start.1 = (f32[2,2,384,128]{3,2,1,0:T(8,128)S(1)}, f32[2,2,384,128]{3,2,1,0:T(8,128)S(1)}, u32[]{:S(2)}, u32[]{:S(2)}) collective-permute-start(f32[2,2,384,128]{3,2,1,0:T(8,128)S(1)} %slice.94), channel_id=1, source_target_pairs={{1,0},{3,2},{5,4},{7,6},{9,8},{11,10},{13,12},{15,14},{17,16},{19,... | collective-permute-start | bytes 2359304 | tf_op jit(solution)/shard_map/ppermute | solution.py:203
  61.0 4.7 %collective-permute-start.2 = (f32[2,3,384,128]{3,2,1,0:T(8,128)S(1)}, f32[2,3,384,128]{3,2,1,0:T(8,128)S(1)}, u32[]{:S(2)}, u32[]{:S(2)}) collective-permute-start(f32[2,3,384,128]{3,2,1,0:T(8,128)S(1)} %slice.97), channel_id=1, source_target_pairs={{0,1},{2,3},{4,5},{6,7},{8,9},{10,11},{12,13},{14,15},{16,17},{18,... | collective-permute-start | bytes 3538952 | tf_op jit(solution)/shard_map/ppermute | solution.py:203
  67.2 21.8 %collective-permute-start.3 = (f32[2,3,128,256]{3,2,1,0:T(8,128)S(1)}, f32[2,3,128,256]{3,2,1,0:T(8,128)S(1)}, u32[]{:S(2)}, u32[]{:S(2)}) collective-permute-start(f32[2,3,128,256]{3,2,1,0:T(8,128)S(1)} %slice.100), channel_id=1, source_target_pairs={{0,2},{2,4},{4,6},{1,3},{3,5},{5,7},{8,10},{10,12},{12,14},{9,11},... | collective-permute-start | bytes 2359304 | tf_op jit(solution)/shard_map/ppermute | solution.py:203
  89.1 1.1 copy-start
  90.3 64.9 %all-gather.2.cloned.1.call-start = ((), (), s32[]{:S(2)}) async-start(), calls=%async_computation.2 | async-start | bytes 1310720 | tf_op jit(solution)/shard_map/all_gather | solution.py:243
Sparse Core Ops, SparseCore 0:
  90.4 33.7 reduce-scatter.1
  127.0 28.0 all-gather.1

commit v2 on v1

--- a/solution.py
+++ b/solution.py
@@ -197,50 +197,258 @@
     )(corner, extended, probe_modes, measured_one, tables)
 
 
-def from_behind(array, axis, by):
-    count = lax.axis_size(axis)
-    pairs = [(i, i + by) for i in range(count) if 0 <= i + by < count]
-    return lax.ppermute(array, axis, pairs)
-
-
-def extend_tile(current, rim_width):
-    below_rim = from_behind(current[:, :, :rim_width, :], "tx", -1)
-    taller = jnp.concatenate([current, below_rim], axis=2)
-    right_rim = from_behind(taller[:, :, :, :rim_width], "ty", -1)
-    return jnp.concatenate([taller, right_rim], axis=3)
-
-
-def return_rims(accumulated, tile_side, rim_width):
-    spilled = from_behind(accumulated[:, :, :, tile_side:], "ty", 1)
-    narrowed = accumulated[:, :, :, :tile_side].at[:, :, :, :rim_width].add(spilled)
-    lower_rim = from_behind(narrowed[:, :, tile_side:, :], "tx", 1)
-    return narrowed[:, :, :tile_side, :].at[:, :, :rim_width, :].add(lower_rim)
-
-
-def on_device(object_slices, probe_modes, corners, measured):
+MESH = pl.DeviceIdType.MESH
+
+
+def meet(neighbours):
+    barrier = pltpu.get_barrier_semaphore()
+    for there, target in neighbours:
+
+        @pl.when(there)
+        def _():
+            pl.semaphore_signal(barrier, inc=1, device_id=target, device_id_type=MESH)
+
+    pl.semaphore_wait(barrier, sum(there.astype(jnp.int32) for there, _ in neighbours))
+
+
+def fetch_kernel(n_tx, n_ty, tile, ext, send_sem, recv_sem):
+    tx, ty = lax.axis_index("tx"), lax.axis_index("ty")
+    side, wide = tile.shape[1], ext.shape[1]
+    rim = wide - side
+    up, left = tx > 0, ty > 0
+    down, right = tx + 1 < n_tx, ty + 1 < n_ty
+    tx_up, ty_left = jnp.maximum(tx - 1, 0), jnp.maximum(ty - 1, 0)
+    tx_down, ty_right = jnp.minimum(tx + 1, n_tx - 1), jnp.minimum(ty + 1, n_ty - 1)
+    meet([
+        (up, {"tx": tx_up}),
+        (down, {"tx": tx_down}),
+        (left, {"ty": ty_left}),
+        (right, {"ty": ty_right}),
+        (up & left, {"tx": tx_up, "ty": ty_left}),
+        (down & right, {"tx": tx_down, "ty": ty_right}),
+    ])
+
+    def rim_copy(slot, source, place, target):
+        return pltpu.make_async_remote_copy(
+            src_ref=source, dst_ref=place, send_sem=send_sem.at[slot], recv_sem=recv_sem.at[slot],
+            device_id=target, device_id_type=MESH,
+        )
+
+    near, far = pl.ds(0, side), pl.ds(side, rim)
+    first = pl.ds(0, rim)
+    copies = [
+        (up, down, rim_copy(0, tile.at[:, first, :], ext.at[:, far, near], {"tx": tx_up}), far, near),
+        (
+            up & left, down & right,
+            rim_copy(1, tile.at[:, first, first], ext.at[:, far, far], {"tx": tx_up, "ty": ty_left}),
+            far, far,
+        ),
+        (left, right, rim_copy(2, tile.at[:, :, first], ext.at[:, near, far], {"ty": ty_left}), near, far),
+    ]
+    for sends, _, copy, _, _ in copies:
+
+        @pl.when(sends)
+        def _():
+            copy.start()
+
+    ext[:, near, near] = tile[...]
+    for _, gets, _, rows, cols in copies:
+
+        @pl.when(jnp.logical_not(gets))
+        def _():
+            ext[:, rows, cols] = jnp.zeros((tile.shape[0], rows.size, cols.size), jnp.float32)
+
+    for sends, gets, copy, _, _ in copies:
+
+        @pl.when(gets)
+        def _():
+            copy.wait_recv()
+
+        @pl.when(sends)
+        def _():
+            copy.wait_send()
+
+
+def extend_tile(tile, rim, n_tx, n_ty):
+    wide = tile.shape[1] + rim
+    vmem = pl.BlockSpec(memory_space=pltpu.VMEM)
+    return pl.pallas_call(
+        functools.partial(fetch_kernel, n_tx, n_ty),
+        out_shape=jax.ShapeDtypeStruct((tile.shape[0], wide, wide), jnp.float32),
+        in_specs=[vmem],
+        out_specs=vmem,
+        scratch_shapes=[pltpu.SemaphoreType.DMA((3,)), pltpu.SemaphoreType.DMA((3,))],
+        compiler_params=pltpu.CompilerParams(collective_id=0, has_side_effects=True),
+        name="fetch_rims",
+    )(tile)
+
+
+def reduce_kernel(
+    n, n_tx, n_ty, acc, tile, out, ty_buf, tx_buf, work, rs_buf, fresh,
+    rim_send, rim_recv, rs_send, rs_recv, ag_send, ag_recv,
+):
+    me, tx, ty = lax.axis_index("scan"), lax.axis_index("tx"), lax.axis_index("ty")
+    side, wide = tile.shape[1], acc.shape[1]
+    rim = wide - side
+    up, left = tx > 0, ty > 0
+    down, right = tx + 1 < n_tx, ty + 1 < n_ty
+    tx_up, ty_left = jnp.maximum(tx - 1, 0), jnp.maximum(ty - 1, 0)
+    tx_down, ty_right = jnp.minimum(tx + 1, n_tx - 1), jnp.minimum(ty + 1, n_ty - 1)
+    peers = [lax.rem(me + d, n) for d in range(1, n)]
+    meet(
+        [
+            (up, {"tx": tx_up}),
+            (down, {"tx": tx_down}),
+            (left, {"ty": ty_left}),
+            (right, {"ty": ty_right}),
+        ]
+        + [(me >= 0, {"scan": peer}) for peer in peers]
+    )
+
+    def rim_copy(slot, source, place, target):
+        return pltpu.make_async_remote_copy(
+            src_ref=source, dst_ref=place, send_sem=rim_send.at[slot], recv_sem=rim_recv.at[slot],
+            device_id=target, device_id_type=MESH,
+        )
+
+    to_right = [
+        rim_copy(slot, acc.at[:, rows, pl.ds(side, rim)], ty_buf.at[:, rows, :], {"ty": ty_right})
+        for slot, rows in enumerate((pl.ds(side, rim), pl.ds(0, side)))
+    ]
+    to_below = rim_copy(2, work.at[:, pl.ds(side, rim), :], tx_buf, {"tx": tx_down})
+
+    @pl.when(right)
+    def _():
+        to_right[0].start()
+        to_right[1].start()
+
+    work[:, side:, :] = acc[:, side:, :side]
+
+    @pl.when(left)
+    def _():
+        to_right[0].wait_recv()
+        work[:, side:, :rim] += ty_buf[:, side:, :]
+
+    @pl.when(down)
+    def _():
+        to_below.start()
+
+    work[:, :side, :] = acc[:, :side, :side]
+
+    @pl.when(left)
+    def _():
+        to_right[1].wait_recv()
+        work[:, :side, :rim] += ty_buf[:, :side, :]
+
+    starts = (rim, 0)
+    counts = ((side - rim) // n, rim // n)
+
+    def rows_of(part, owner):
+        return pl.ds(pl.multiple_of(starts[part] + owner * counts[part], 8), counts[part])
+
+    def share_copy(part, d):
+        return pltpu.make_async_remote_copy(
+            src_ref=work.at[:, rows_of(part, peers[d]), :],
+            dst_ref=rs_buf.at[d, :, pl.ds(part * counts[0], counts[part]), :],
+            send_sem=rs_send.at[part, d], recv_sem=rs_recv.at[part, d],
+            device_id={"scan": peers[d]}, device_id_type=MESH,
+        )
+
+    def fresh_copy(part, d):
+        return pltpu.make_async_remote_copy(
+            src_ref=fresh.at[:, pl.ds(part * counts[0], counts[part]), :],
+            dst_ref=out.at[:, rows_of(part, me), :],
+            send_sem=ag_send.at[part, d], recv_sem=ag_recv.at[part, d],
+            device_id={"scan": peers[d]}, device_id_type=MESH,
+        )
+
+    def finish(part):
+        own = rows_of(part, me)
+        kept = pl.ds(part * counts[0], counts[part])
+        total = work[:, own, :]
+        for d in range(n - 1):
+            share_copy(part, d).wait_recv()
+            total = total + rs_buf[d, :, kept, :]
+        for p in range(tile.shape[0]):
+            base = p // 2 * 3
+            new = tile[p, own, :] - step_size * total[base + p % 2] / (total[base + 2] + 1.0)
+            fresh[p, kept, :] = new
+            out[p, own, :] = new
+        for d in range(n - 1):
+            fresh_copy(part, d).start()
+
+    for d in range(n - 1):
+        share_copy(0, d).start()
+
+    @pl.when(up)
+    def _():
+        to_below.wait_recv()
+        work[:, :rim, :] += tx_buf[...]
+
+    for d in range(n - 1):
+        share_copy(1, d).start()
+    finish(0)
+    finish(1)
+    for part in range(2):
+        for d in range(n - 1):
+            fresh_copy(part, d).wait_recv()
+    for part in range(2):
+        for d in range(n - 1):
+            share_copy(part, d).wait_send()
+            fresh_copy(part, d).wait_send()
+
+    @pl.when(right)
+    def _():
+        to_right[0].wait_send()
+        to_right[1].wait_send()
+
+    @pl.when(down)
+    def _():
+        to_below.wait_send()
+
+
+def reduce_and_update(acc, tile, n, n_tx, n_ty):
+    planes, wide, _ = acc.shape
+    side = tile.shape[1]
+    rim = wide - side
+    own = side // n
+    vmem = pl.BlockSpec(memory_space=pltpu.VMEM)
+    dma = pltpu.SemaphoreType.DMA
+    return pl.pallas_call(
+        functools.partial(reduce_kernel, n, n_tx, n_ty),
+        out_shape=jax.ShapeDtypeStruct(tile.shape, jnp.float32),
+        in_specs=[vmem, vmem],
+        out_specs=vmem,
+        scratch_shapes=[
+            pltpu.VMEM((planes, wide, rim), jnp.float32),
+            pltpu.VMEM((planes, rim, side), jnp.float32),
+            pltpu.VMEM((planes, wide, side), jnp.float32),
+            pltpu.VMEM((n - 1, planes, own, side), jnp.float32),
+            pltpu.VMEM((tile.shape[0], own, side), jnp.float32),
+            dma((3,)), dma((3,)),
+            dma((2, n - 1)), dma((2, n - 1)), dma((2, n - 1)), dma((2, n - 1)),
+        ],
+        compiler_params=pltpu.CompilerParams(collective_id=1, has_side_effects=True),
+        name="reduce_update",
+    )(acc, tile)
+
+
+def on_device(n_scan, n_tx, n_ty, object_slices, probe_modes, corners, measured):
     layers = object_slices.shape[0]
     tile_side = object_slices.shape[2]
     pixels = probe_modes.shape[-1]
-    rim_width = pixels // 2
     positions = corners.shape[2]
-    share_rows = tile_side // lax.axis_size("scan")
-    wide = tile_side + rim_width
     tables = jnp.asarray(dft_tables(pixels))
-    current = object_slices
-    extended = extend_tile(current, rim_width).reshape(2 * layers, wide, wide)
+    tile = object_slices.reshape(2 * layers, tile_side, tile_side)
+    extended = extend_tile(tile, pixels // 2, n_tx, n_ty)
     accumulated = sum(
         position_terms(
             corners[0, 0, position], extended, probe_modes, measured[0, 0, position], tables
         )
         for position in range(positions)
-    ).reshape(layers, 3, wide, wide)
-    shared = lax.psum_scatter(
-        return_rims(accumulated, tile_side, rim_width), "scan", scatter_dimension=2, tiled=True
-    )
-    row_first = lax.axis_index("scan") * share_rows
-    own_rows = lax.dynamic_slice_in_dim(current, row_first, share_rows, 2)
-    own_new = own_rows - step_size * shared[:, :2] / (shared[:, 2:3] + 1.0)
-    return lax.all_gather(own_new, "scan", axis=2, tiled=True)
+    )
+    updated = reduce_and_update(accumulated, tile, n_scan, n_tx, n_ty)
+    return updated.reshape(object_slices.shape)
 
 
 def solution(mesh):
@@ -250,6 +458,11 @@
         P("tx", "ty", "scan", None),
         P("tx", "ty", "scan", None, None),
     )
+    sizes = (mesh.shape["scan"], mesh.shape["tx"], mesh.shape["ty"])
     return jax.shard_map(
-        on_device, mesh=mesh, in_specs=placed, out_specs=P(None, None, "tx", "ty"), check_vma=False
-    )
+        functools.partial(on_device, *sizes),
+        mesh=mesh,
+        in_specs=placed,
+        out_specs=P(None, None, "tx", "ty"),
+        check_vma=False,
+    )

time: 167 us -> 120 us (0.72); the launches traced: 164 us -> 120 us
  waiting for transfers between devices: 96.9 us -> 0 us
  Pallas kernels: 30.2 us -> 118 us
  between operations: 13.5 us -> 0.02 us
  starting transfers between devices: 9.8 us -> 0 us
  local copies, waits for them, and re-layouts: 8.07 us -> 2.29 us
  other arithmetic: 5.71 us -> 0 us
    pallas_call x0 -> x2, Pallas kernels: none -> 87.4 us  [the longest x1 68.4 us: reduce_and_update(): pl.pallas_call(functools.partial(reduce_kernel, n, n_tx, n_ty), out_shape...]
    ppermute x4 -> x0, waiting for transfers between devices: 34.7 us -> none  [from_behind(): return lax.ppermute(array, axis, pairs)]
    reduce_scatter x1 -> x0, waiting for transfers between devices: 33.9 us -> none  [on_device(): lax.psum_scatter(return_rims(accumulated, tile_side, rim_width), 'scan',...]
    all_gather x1 -> x0, waiting for transfers between devices: 28.3 us -> none  [on_device(): return lax.all_gather(own_new, 'scan', axis=2, tiled=True)]
    ppermute x4 -> x0, starting transfers between devices: 9.76 us -> none  [from_behind(): return lax.ppermute(array, axis, pairs)]
    slice x6 -> x0, local copies, waits for them, and re-layouts: 4.54 us -> none  [the longest x1 1.82 us: return_rims(): accumulated[:, :, :, :tile_side].at[:, :, :, :rim_width].add(spilled)]
    sub x1 -> x0, other arithmetic: 1.71 us -> none  [on_device(): own_new = own_rows - step_size * shared[:, :2] / (shared[:, 2:3] + 1.0)]
    unnamed x6 -> x1, local copies, waits for them, and re-layouts: 3.5 us -> 2.29 us
  transfers between devices with their start and end apart: 6 -> 0, of which waited for: 6 -> 0; matrix products, arithmetic and copies ran while one was open for 1% -> 0% of each run, Pallas kernels for 0% -> 0%
where the time goes in v2:
time: 120 us
  Pallas kernels  118 us (98%)
  local copies, waits for them, and re-layouts  2.29 us (2%)
    pallas_call x1, Pallas kernels, reduce_and_update(): pl.pallas_call(functools.partial(reduce_kernel, n, n_tx, n_ty), out_shape...  68.4 us
    pallas_call x1, Pallas kernels, position_terms(): pl.pallas_call(position_kernel, out_shape=jax.ShapeDtypeStruct((6, wide,...  30.3 us
    pallas_call x1, Pallas kernels, extend_tile(): pl.pallas_call(functools.partial(fetch_kernel, n_tx, n_ty), out_shape=jax...  19 us

profile of v2, /device:TPU:13, one launch (start us, length us, event | category | flops | bytes accessed | tf_op | source)
XLA Modules:
  0.0 119.9 jit_solution(10011211855979939111)
XLA Ops:
  0.0 19.0 %fetch_rims.1.ext = f32[4,384,384]{2,1,0:T(8,128)} custom-call(f32[4,256,256]{2,1,0:T(8,128)} %bitcast.4), custom_call_target="tpu_custom_call" | custom-call | tf_op jit(solution)/shard_map/fetch_rims/pallas_call | solution.py:275
  19.0 30.3 %position_terms.1.acc = f32[6,384,384]{2,1,0:T(8,128)} custom-call(s32[2]{0:T(128)} %bitcast.8, f32[4,384,384]{2,1,0:T(8,128)} %fetch_rims.1.ext, f32[2,8,256,256]{3,2,1,0:T(8,128)} %probe.1, f32[256,256]{1,0:T(8,128)} %bitcast.7, bf16[8,256,256]{2,1,0:T(8,128)(2,1)} %constant.2.clone.tables), custom_call_target="tpu_custom_call" | custom-call | tf_op jit(solution)/shard_map/position_terms/pallas_call | solution.py:182
  49.2 68.4 %reduce_update.1 = f32[4,256,256]{2,1,0:T(8,128)} custom-call(f32[6,384,384]{2,1,0:T(8,128)} %position_terms.1.acc, f32[4,256,256]{2,1,0:T(8,128)} %bitcast.5), custom_call_target="tpu_custom_call" | custom-call | tf_op jit(solution)/shard_map/reduce_update/pallas_call | solution.py:417
  117.7 2.3 %copy.7 = f32[2,2,256,256]{3,2,1,0:T(8,128)} copy(f32[2,2,256,256]{3,2,1,0:T(8,128)} %bitcast.6) | data formatting | bytes 2097152

commit v3 on v2

--- a/solution.py
+++ b/solution.py
@@ -135,7 +135,7 @@
         misfit[h:] += f_odd[:h] * f_odd[:h] + f_odd[h:] * f_odd[h:]
         return 0
 
-    lax.fori_loop(0, modes, forward, 0)
+    lax.fori_loop(0, modes, forward, 0, unroll=2)
 
     def backward(m, _):
         m_even, m_odd = 2.0 * misfit[:h], 2.0 * misfit[h:]
@@ -167,7 +167,7 @@
         sums[1] += wr * bi - wi * br
         return 0
 
-    lax.fori_loop(0, modes, backward, 0)
+    lax.fori_loop(0, modes, backward, 0, unroll=2)
     padded[...] = jnp.zeros_like(padded)
     for p in range(6):
         padded[:n, :n] = sums[p]

time: 120 us -> 116 us (0.967)
  Pallas kernels: 118 us -> 114 us
    pallas_call x1, Pallas kernels: 30.3 us -> 26.5 us  [position_terms(): pl.pallas_call(position_kernel, out_shape=jax.ShapeDtypeStruct((6, wide,...]
where the time goes in v3:
time: 116 us
  Pallas kernels  114 us (98%)
  local copies, waits for them, and re-layouts  2.29 us (2%)
    pallas_call x1, Pallas kernels, reduce_and_update(): pl.pallas_call(functools.partial(reduce_kernel, n, n_tx, n_ty), out_shape...  68.4 us
    pallas_call x1, Pallas kernels, position_terms(): pl.pallas_call(position_kernel, out_shape=jax.ShapeDtypeStruct((6, wide,...  26.5 us
    pallas_call x1, Pallas kernels, extend_tile(): pl.pallas_call(functools.partial(fetch_kernel, n_tx, n_ty), out_shape=jax...  19 us

profile of v3, /device:TPU:13, one launch (start us, length us, event | category | flops | bytes accessed | tf_op | source)
XLA Modules:
  0.0 116.1 jit_solution(14433068906827489526)
XLA Ops:
  0.0 19.0 %fetch_rims.1.ext = f32[4,384,384]{2,1,0:T(8,128)} custom-call(f32[4,256,256]{2,1,0:T(8,128)} %bitcast.4), custom_call_target="tpu_custom_call" | custom-call | tf_op jit(solution)/shard_map/fetch_rims/pallas_call | solution.py:275
  19.0 26.5 %position_terms.1.acc = f32[6,384,384]{2,1,0:T(8,128)} custom-call(s32[2]{0:T(128)} %bitcast.8, f32[4,384,384]{2,1,0:T(8,128)} %fetch_rims.1.ext, f32[2,8,256,256]{3,2,1,0:T(8,128)} %probe.1, f32[256,256]{1,0:T(8,128)} %bitcast.7, bf16[8,256,256]{2,1,0:T(8,128)(2,1)} %constant.2.clone.tables), custom_call_target="tpu_custom_call" | custom-call | tf_op jit(solution)/shard_map/position_terms/pallas_call | solution.py:182
  45.4 68.4 %reduce_update.1 = f32[4,256,256]{2,1,0:T(8,128)} custom-call(f32[6,384,384]{2,1,0:T(8,128)} %position_terms.1.acc, f32[4,256,256]{2,1,0:T(8,128)} %bitcast.5), custom_call_target="tpu_custom_call" | custom-call | tf_op jit(solution)/shard_map/reduce_update/pallas_call | solution.py:417
  113.9 2.3 %copy.7 = f32[2,2,256,256]{3,2,1,0:T(8,128)} copy(f32[2,2,256,256]{3,2,1,0:T(8,128)} %bitcast.6) | data formatting | bytes 2097152
